TPU v7x, 128 devices: a whole 4x4x4 slice. The times are simulated.
128 devices in a mesh: grp: 8 (over z, core), sub: 16 (over x, y).
Axes of the slice: x: 4, y: 4, z: 4, core: 2. Of those that a mesh axis runs over, the one named last changes fastest.
Arguments:
- rhs: float32 [96, 131072], P(None, ('grp', 'sub')), may hold values from -13 to 13
- blocks: bfloat16 [16384, 6656], P(('grp', 'sub')), may hold values from -0.05 to 0.45, as said below
- owners: int32 [16384, 1], P(('grp', 'sub')), may hold values from 0 to 7; in each aligned block of 128 rows (0 to 127, 128 to 255, ...) at most 48 rows name the same one
- conn: int32 [16384, 27], P(('grp', 'sub')), may hold values from 0 to 16383, as said below
Outputs:
- solution: float32 [96, 131072], P(None, ('grp', 'sub'))
- residual: float32 [96, 131072], P(None, ('grp', 'sub'))
Inputs may be any that keep to these rules, and one draw needn't show every extreme that they name: `blocks`: entries at positions 6561 and beyond are zero. `owners`: in each device's 128 rows at most 48 name the same column. `conn`: A column's nodes form layers of 128 nodes, node n in layer n // 128. An element in the rows of the device at position s along sub touches three consecutive layers, all within nodes s * 1024 to (s + 1) * 1024 + 2 * 128 - 1 of its column (within the column).
All inputs are finite; a program needn't handle non-finite values.
Results may differ from a plain program's by a relative error of at most 0.0075.
Values may be sent and summed in bfloat16 or wider, within the bound.
A program may use at most 192 MiB of HBM per device.

v0:
```python
import jax
import jax.numpy as jnp
from jax import lax
from jax.sharding import PartitionSpec as P

STEPS = 2


epsilon = 1e-06


def passed_along(block, axis, distance):
    devices = range(lax.axis_size(axis))
    route = [(i - distance, i) for i in devices if i - distance in devices]
    return lax.ppermute(block, axis, route)


def place_blocks(blocks, owners, conn, groups, capacity):
    owner_group = owners[:, 0]
    onehot = (owner_group[:, None] == jnp.arange(groups, dtype=jnp.int32)[None, :]).astype(
        jnp.int32
    )
    before = jnp.cumsum(onehot, axis=0) - onehot
    position = jnp.sum(before * onehot, axis=1)
    target = owner_group * capacity + position
    send_blocks = (
        jnp.zeros((groups * capacity, blocks.shape[1]), blocks.dtype).at[target].set(blocks)
    )
    send_links = jnp.zeros((groups * capacity, conn.shape[1]), jnp.int32).at[target].set(conn)
    return (send_blocks.reshape(groups, capacity, -1), send_links.reshape(groups, capacity, -1))


def window_product(matrix_groups, link_groups, field):
    rows = field.shape[0]
    window = field.shape[1]
    places = jnp.arange(window, dtype=jnp.int32)

    def one_group(acc, pair):
        matrix, links = pair
        slot_count = matrix.shape[0]
        selector = (links[:, None] == places[None, :]).astype(jnp.bfloat16)
        picked = jnp.einsum(
            "rw,lw->rl", field, selector, preferred_element_type=jnp.float32
        ).astype(jnp.bfloat16)
        picked = picked.reshape(3, rows // 3, slot_count, 27)
        result = jnp.einsum("spcqd,cosp->dosq", matrix, picked, preferred_element_type=jnp.float32)
        result = result.reshape(rows, slot_count * 27)
        high_part = result.astype(jnp.bfloat16)
        low_part = (result - high_part.astype(jnp.float32)).astype(jnp.bfloat16)
        acc = acc + jnp.dot(high_part, selector, preferred_element_type=jnp.float32)
        acc = acc + jnp.dot(low_part, selector, preferred_element_type=jnp.float32)
        return (acc, None)

    start = jnp.zeros((rows, window), jnp.float32)
    acc, unused = lax.scan(one_group, start, (matrix_groups, link_groups))
    return acc


def column_sums(first, second):
    return jnp.sum((first * second).reshape(3, -1, first.shape[1]), axis=(0, 2))


def update(solution, residual, image, along, energy):
    alpha = along / (energy + epsilon)
    scale_rows = jnp.tile(alpha, 3)[:, None]
    return (solution + scale_rows * residual, residual - scale_rows * image)


def shards(rhs, blocks, owners, conn):
    groups = lax.axis_size("grp")
    held = blocks.shape[0]
    capacity = max(2, 3 * held // 8)
    send_blocks, send_links = place_blocks(blocks, owners, conn, groups, capacity)
    got_blocks, got_links = (
        lax.all_to_all(send_blocks, "grp", split_axis=0, concat_axis=0, tiled=True),
        lax.all_to_all(send_links, "grp", split_axis=0, concat_axis=0, tiled=True),
    )
    matrix_groups = got_blocks[:, :, :6561].reshape(groups, capacity, 27, 3, 27, 3)
    residual = rhs
    solution = jnp.zeros(rhs.shape, jnp.float32)
    own_count = rhs.shape[1]
    band_width = 2 * held
    local_links = jnp.clip(
        got_links - lax.axis_index("sub") * own_count, 0, own_count + band_width - 1
    ).astype(jnp.int32)
    link_groups = local_links.reshape(groups, capacity * 27)
    for step in range(STEPS):
        rounded = residual.astype(jnp.bfloat16)
        upper = passed_along(rounded[:, :band_width], "sub", -1)
        field = jnp.concatenate([rounded, upper], axis=1)
        partial_sum = window_product(matrix_groups, link_groups, field)
        incoming = passed_along(partial_sum[:, own_count:], "sub", 1)
        image = partial_sum[:, :own_count] + jnp.pad(
            incoming, ((0, 0), (0, own_count - band_width))
        )
        along, energy = lax.psum(
            (column_sums(residual, image), column_sums(image, image)), ("grp", "sub")
        )
        solution, residual = update(solution, residual, image, along, energy)
    return (solution, residual)


def solution(mesh):
    return jax.shard_map(
        shards,
        mesh=mesh,
        in_specs=(
            P(None, ("grp", "sub")),
            P(("grp", "sub"), None),
            P(("grp", "sub"), None),
            P(("grp", "sub"), None),
        ),
        out_specs=(P(None, ("grp", "sub")), P(None, ("grp", "sub"))),
        check_vma=False,
    )
```

profile of v0, /device:TPU:2, one launch (start us, length us, event | category | flops | bytes accessed | tf_op | source)
XLA Modules:
  0.0 515.6 jit_solution(13757841406392980905)
XLA Ops:
  5.7 5.3 %all-to-all-start = ((s32[8,1,1296]{2,1,0:T(1,128)}), s32[8,1,1296]{2,1,0:T(1,128)S(1)}, u32[]{:S(2)}, u32[]{:S(2)}) async-start(s32[8,1,1296]{2,1,0:T(1,128)} %reshape.81), calls=%async_computation | async-start | bytes 90112 | tf_op jit(solution)/shard_map/all_to_all | solution.py:76
  11.0 6.9 %scatter_custom_fusion.1 = bf16[384,6656]{1,0:T(8,128)(2,1)} fusion(s32[128]{0:T(128)S(1)} %fusion.50, bf16[128,6656]{1,0:T(8,128)(2,1)} %param.9, bf16[]{:T(256)} %constant.23.clone.1), kind=kCustom, calls=%fused_computation.46 | custom fusion | bytes 5112320 | tf_op jit(solution)/shard_map/scatter | solution.py:27
  18.0 4.9 all-to-all-start.1
  23.0 5.1 collective-permute-start
  30.5 52.1 %all-to-all-done.1 = bf16[8,48,6656]{2,1,0:T(8,128)(2,1)} async-done(((bf16[8,48,6656]{2,1,0:T(8,128)(2,1)}), bf16[8,48,6656]{2,1,0:T(8,128)(2,1)}, u32[]{:S(2)}, u32[]{:S(2)}) %all-to-all-start.1) | async-done | bytes 5111840 | tf_op jit(solution)/shard_map/all_to_all | solution.py:75
  82.5 14.8 %copy.45 = bf16[8,48,6561]{1,0,2:T(8,128)(2,1)} copy(bf16[8,48,6561]{2,1,0:T(8,128)(2,1)} %bitcast.44) | data formatting | bytes 10077696
  97.3 35.7 %copy.35 = bf16[8,48,27,3,27,3]{4,2,3,5,1,0:T(8,128)(2,1)} copy(bf16[8,48,27,3,27,3]{1,0,5,4,3,2:T(8,128)(2,1)} %bitcast.67) | data formatting | bytes 10077696
  133.0 112.3 %while.22 = (s32[]{:T(128)}, f32[96,1280]{1,0:T(8,128)}, s32[8,1296]{1,0:T(8,128)}, bf16[96,1280]{1,0:T(8,128)(2,1)S(1)}, bf16[8,48,27,3,27,3]{4,2,3,5,1,0:T(8,128)(2,1)}, /*index=5*/s32[]{:T(128)}, s32[]{:T(128)}) while((s32[]{:T(128)}, f32[96,1280]{1,0:T(8,128)}, s32[8,1296]{1,0:T(8,128)}, bf16[96,1280]{1,0:T(8,128)(2,1)S(1)}, ...), condition=%wide.region_5.6_spmd.clone, body=%wide.region_4.5_spmd.clone.sunk | while | flops 981762048 | bytes 10256283 | solution.py:55
  137.0 2.8 fusion.75
  150.2 2.8 fusion.75
  155.4 2.6 fusion.76
  164.3 2.8 fusion.75
  178.5 2.8 fusion.75
  192.7 2.8 fusion.75
  206.8 2.8 fusion.75
  221.0 2.8 fusion.75
  235.2 2.8 fusion.75
  246.2 3.5 collective-permute-start.1
  249.6 5.1 collective-permute-done.1
  256.2 62.6 %all-reduce.3 = (f32[32]{0:T(128)S(1)}, f32[32]{0:T(128)S(1)}) all-reduce(f32[32]{0:T(128)S(1)} %reduce_sum.62, f32[32]{0:T(128)S(1)} %reduce_sum.82), channel_id=1, replica_groups=mesh['grp'=8,'sub'=16] {'grp','sub'}, use_global_device_ids=true, to_apply=%region_8.9 | all-reduce | flops 64 | bytes 512 | tf_op jit(solution)/shard_map/psum | solution.py:96
  320.7 4.7 collective-permute-start.2
  327.0 112.3 %while.23 = (s32[]{:T(128)}, f32[96,1280]{1,0:T(8,128)}, s32[8,1296]{1,0:T(8,128)}, bf16[96,1280]{1,0:T(8,128)(2,1)S(1)}, bf16[8,48,27,3,27,3]{4,2,3,5,1,0:T(8,128)(2,1)}, /*index=5*/s32[]{:T(128)}, s32[]{:T(128)}) while((s32[]{:T(128)}, f32[96,1280]{1,0:T(8,128)}, s32[8,1296]{1,0:T(8,128)}, bf16[96,1280]{1,0:T(8,128)(2,1)S(1)}, ...), condition=%wide.region_13.14_spmd.clone, body=%wide.region_12.13_spmd.clone.sunk | while | flops 981762048 | bytes 10256283 | solution.py:55
  331.0 2.8 fusion.83
  344.2 2.8 fusion.83
  358.3 2.8 fusion.83
  372.5 2.8 fusion.83
  386.7 2.8 fusion.83
  400.8 2.8 fusion.83
  415.0 2.8 fusion.83
  429.2 2.8 fusion.83
  442.1 7.0 %collective-permute-done.3 = f32[96,256]{1,0:T(8,128)S(1)} collective-permute-done((f32[96,256]{1,0:T(8,128)S(1)}, f32[96,256]{1,0:T(8,128)S(1)}, u32[]{:S(2)}, u32[]{:S(2)}) %collective-permute-start.3) | collective-permute-done | bytes 98336 | tf_op jit(solution)/shard_map/ppermute | solution.py:15
  450.6 62.8 %all-reduce.2 = (f32[32]{0:T(128)S(1)}, f32[32]{0:T(128)S(1)}) all-reduce(f32[32]{0:T(128)S(1)} %reduce_sum.85, f32[32]{0:T(128)S(1)} %reduce_sum.88), channel_id=1, replica_groups=mesh['grp'=8,'sub'=16] {'grp','sub'}, use_global_device_ids=true, to_apply=%region_16.17 | all-reduce | flops 64 | bytes 512 | tf_op jit(solution)/shard_map/psum | solution.py:96
  (158 shorter events, 196.2 us)
Async XLA Ops:
  5.7 12.3 %all-to-all-start = ((s32[8,1,1296]{2,1,0:T(1,128)}), s32[8,1,1296]{2,1,0:T(1,128)S(1)}, u32[]{:S(2)}, u32[]{:S(2)}) async-start(s32[8,1,1296]{2,1,0:T(1,128)} %reshape.81), calls=%async_computation | async-start | bytes 90112 | tf_op jit(solution)/shard_map/all_to_all | solution.py:76
  18.0 4.9 copy-start
  18.0 64.5 %all-to-all-start.1 = ((bf16[8,48,6656]{2,1,0:T(8,128)(2,1)}), bf16[8,48,6656]{2,1,0:T(8,128)(2,1)}, u32[]{:S(2)}, u32[]{:S(2)}) async-start(bf16[8,48,6656]{2,1,0:T(8,128)(2,1)} %bitcast.68), calls=%async_computation.1 | async-start | bytes 10223616 | tf_op jit(solution)/shard_map/all_to_all | solution.py:75
  23.0 7.5 %collective-permute-start = (bf16[96,256]{1,0:T(8,128)(2,1)S(1)}, bf16[96,256]{1,0:T(8,128)(2,1)S(1)}, u32[]{:S(2)}, u32[]{:S(2)}) collective-permute-start(bf16[96,256]{1,0:T(8,128)(2,1)S(1)} %slice.28), channel_id=1, source_target_pairs={{1,0},{2,1},{3,2},{4,3},{5,4},{6,5},{7,6},{8,7},{9,8},{10,9},{11,1... | collective-permute-start | bytes 147464 | tf_op jit(solution)/shard_map/ppermute | solution.py:15
  246.2 8.6 %collective-permute-start.1 = (f32[96,256]{1,0:T(8,128)S(1)}, f32[96,256]{1,0:T(8,128)S(1)}, u32[]{:S(2)}, u32[]{:S(2)}) collective-permute-start(f32[96,256]{1,0:T(8,128)S(1)} %slice.24), channel_id=1, source_target_pairs={{0,1},{1,2},{2,3},{3,4},{4,5},{5,6},{6,7},{7,8},{8,9},{9,10},{10,1... | collective-permute-start | bytes 294920 | tf_op jit(solution)/shard_map/ppermute | solution.py:15
  320.7 6.3 %collective-permute-start.2 = (bf16[96,256]{1,0:T(8,128)(2,1)S(1)}, bf16[96,256]{1,0:T(8,128)(2,1)S(1)}, u32[]{:S(2)}, u32[]{:S(2)}) collective-permute-start(bf16[96,256]{1,0:T(8,128)(2,1)S(1)} %slice.30), channel_id=1, source_target_pairs={{1,0},{2,1},{3,2},{4,3},{5,4},{6,5},{7,6},{8,7},{9,8},{10,9},{11,1... | collective-permute-start | bytes 147464 | tf_op jit(solution)/shard_map/ppermute | solution.py:15
  440.2 8.9 %collective-permute-start.3 = (f32[96,256]{1,0:T(8,128)S(1)}, f32[96,256]{1,0:T(8,128)S(1)}, u32[]{:S(2)}, u32[]{:S(2)}) collective-permute-start(f32[96,256]{1,0:T(8,128)S(1)} %slice.27), channel_id=1, source_target_pairs={{0,1},{1,2},{2,3},{3,4},{4,5},{5,6},{6,7},{7,8},{8,9},{9,10},{10,1... | collective-permute-start | bytes 294920 | tf_op jit(solution)/shard_map/ppermute | solution.py:15
where the time goes:
time: 520 us; the launch traced here: 516 us
  matrix products  147 us (28%)
  local copies, waits for them, and re-layouts  141 us (27%)
  blocking collectives  125 us (24%)
  waiting for transfers between devices  65.7 us (13%)
  starting transfers between devices  25.4 us (5%)
  other arithmetic  9.83 us (2%)
    psum x2, blocking collectives, shards(): lax.psum((column_sums(residual, image), column_sums(image, image)), ('grp...  125 us
    unnamed x7, local copies, waits for them, and re-layouts  52.2 us
    all_to_all x1, waiting for transfers between devices, shards(): lax.all_to_all(send_blocks, 'grp', split_axis=0, concat_axis=0, tiled=True)  52.1 us
    dot_general x16, matrix products, one_group(): jnp.einsum('spcqd,cosp->dosq', matrix, picked, preferred_element_type=jnp...  44.9 us
    dot_general x16, matrix products, one_group(): acc = acc + jnp.dot(high_part, selector, preferred_element_type=jnp.float32)  39.2 us
    dot_general x16, matrix products, one_group(): acc = acc + jnp.dot(low_part, selector, preferred_element_type=jnp.float32)  37.2 us
    reshape x16, local copies, waits for them, and re-layouts, one_group(): picked = picked.reshape(3, rows // 3, slot_count, 27)  26.4 us
    dot_general x16, matrix products, one_group(): jnp.einsum('rw,lw->rl', field, selector, preferred_element_type=jnp.float32)  25.1 us
  transfers between devices with their start and end apart: 6, of which 4 were waited for; matrix products, arithmetic and copies ran while one was open for 2% of the time, Pallas kernels for 0%

commit v1 on v0

--- a/solution.py
+++ b/solution.py
@@ -56,6 +56,15 @@
     return acc
 
 
+def total_over_devices(value):
+    axes = ("grp", "sub")
+    count = lax.axis_size(axes)
+    for bit in range(count.bit_length() - 1):
+        pairs = [(i, i ^ (1 << bit)) for i in range(count)]
+        value = value + lax.ppermute(value, axes, pairs)
+    return value
+
+
 def column_sums(first, second):
     return jnp.sum((first * second).reshape(3, -1, first.shape[1]), axis=(0, 2))
 
@@ -93,9 +102,10 @@
         image = partial_sum[:, :own_count] + jnp.pad(
             incoming, ((0, 0), (0, own_count - band_width))
         )
-        along, energy = lax.psum(
-            (column_sums(residual, image), column_sums(image, image)), ("grp", "sub")
+        sums = total_over_devices(
+            jnp.stack([column_sums(residual, image), column_sums(image, image)])
         )
+        along, energy = sums[0], sums[1]
         solution, residual = update(solution, residual, image, along, energy)
     return (solution, residual)
 

time: 520 us -> 448 us (0.86)
  blocking collectives: 125 us -> 0 us
  waiting for transfers between devices: 65.7 us -> 113 us
  starting transfers between devices: 25.4 us -> 32 us
    psum x2 -> x0, blocking collectives: 125 us -> none  [shards(): lax.psum((column_sums(residual, image), column_sums(image, image)), ('grp...]
    ppermute x0 -> x14, waiting for transfers between devices: none -> 46.1 us  [total_over_devices(): value = value + lax.ppermute(value, axes, pairs)]
    ppermute x0 -> x14, starting transfers between devices: none -> 8.5 us  [total_over_devices(): value = value + lax.ppermute(value, axes, pairs)]
  transfers between devices with their start and end apart: 6 -> 20, of which waited for: 4 -> 18; matrix products, arithmetic and copies ran while one was open for 2% -> 2% of each run, Pallas kernels for 0% -> 0%
where the time goes in v1:
time: 448 us; the launch traced here: 444 us
  matrix products  147 us (33%)
  local copies, waits for them, and re-layouts  141 us (31%)
  waiting for transfers between devices  113 us (25%)
  starting transfers between devices  32 us (7%)
  other arithmetic  9.93 us (2%)
    unnamed x7, local copies, waits for them, and re-layouts  52.2 us
    all_to_all x1, waiting for transfers between devices, shards(): lax.all_to_all(send_blocks, 'grp', split_axis=0, concat_axis=0, tiled=True)  52.1 us
    ppermute x14, waiting for transfers between devices, total_over_devices(): value = value + lax.ppermute(value, axes, pairs)  46.1 us
    dot_general x16, matrix products, one_group(): jnp.einsum('spcqd,cosp->dosq', matrix, picked, preferred_element_type=jnp...  44.9 us
    dot_general x16, matrix products, one_group(): acc = acc + jnp.dot(high_part, selector, preferred_element_type=jnp.float32)  39.2 us
    dot_general x16, matrix products, one_group(): acc = acc + jnp.dot(low_part, selector, preferred_element_type=jnp.float32)  37.2 us
    reshape x16, local copies, waits for them, and re-layouts, one_group(): picked = picked.reshape(3, rows // 3, slot_count, 27)  26.4 us
    dot_general x16, matrix products, one_group(): jnp.einsum('rw,lw->rl', field, selector, preferred_element_type=jnp.float32)  25.1 us
  transfers between devices with their start and end apart: 20, of which 18 were waited for; matrix products, arithmetic and copies ran while one was open for 2% of the time, Pallas kernels for 0%

profile of v1, /device:TPU:2, one launch (start us, length us, event | category | flops | bytes accessed | tf_op | source)
XLA Modules:
  0.0 444.4 jit_solution(16927315093082586210)
XLA Ops:
  5.7 5.3 %all-to-all-start = ((s32[8,1,1296]{2,1,0:T(1,128)}), s32[8,1,1296]{2,1,0:T(1,128)S(1)}, u32[]{:S(2)}, u32[]{:S(2)}) async-start(s32[8,1,1296]{2,1,0:T(1,128)} %reshape.79), calls=%async_computation | async-start | bytes 90112 | tf_op jit(solution)/shard_map/all_to_all | solution.py:85
  11.0 6.9 %scatter_custom_fusion.1 = bf16[384,6656]{1,0:T(8,128)(2,1)} fusion(s32[128]{0:T(128)S(1)} %fusion.50, bf16[128,6656]{1,0:T(8,128)(2,1)} %param.9, bf16[]{:T(256)} %constant.23.clone.1), kind=kCustom, calls=%fused_computation.46 | custom fusion | bytes 5112320 | tf_op jit(solution)/shard_map/scatter | solution.py:27
  18.0 4.9 %all-to-all-start.1 = ((bf16[8,48,6656]{2,1,0:T(8,128)(2,1)}), bf16[8,48,6656]{2,1,0:T(8,128)(2,1)}, u32[]{:S(2)}, u32[]{:S(2)}) async-start(bf16[8,48,6656]{2,1,0:T(8,128)(2,1)} %bitcast.76), calls=%async_computation.1 | async-start | bytes 10223616 | tf_op jit(solution)/shard_map/all_to_all | solution.py:84
  23.0 5.1 %collective-permute-start = (bf16[96,256]{1,0:T(8,128)(2,1)S(1)}, bf16[96,256]{1,0:T(8,128)(2,1)S(1)}, u32[]{:S(2)}, u32[]{:S(2)}) collective-permute-start(bf16[96,256]{1,0:T(8,128)(2,1)S(1)} %slice.44), channel_id=1, source_target_pairs={{1,0},{2,1},{3,2},{4,3},{5,4},{6,5},{7,6},{8,7},{9,8},{10,9},{11,1... | collective-permute-start | bytes 147464 | tf_op jit(solution)/shard_map/ppermute | solution.py:15
  30.5 52.1 %all-to-all-done.1 = bf16[8,48,6656]{2,1,0:T(8,128)(2,1)} async-done(((bf16[8,48,6656]{2,1,0:T(8,128)(2,1)}), bf16[8,48,6656]{2,1,0:T(8,128)(2,1)}, u32[]{:S(2)}, u32[]{:S(2)}) %all-to-all-start.1) | async-done | bytes 5111840 | tf_op jit(solution)/shard_map/all_to_all | solution.py:84
  82.5 14.8 %copy.45 = bf16[8,48,6561]{1,0,2:T(8,128)(2,1)} copy(bf16[8,48,6561]{2,1,0:T(8,128)(2,1)} %bitcast.52) | data formatting | bytes 10077696
  97.3 35.7 %copy.35 = bf16[8,48,27,3,27,3]{4,2,3,5,1,0:T(8,128)(2,1)} copy(bf16[8,48,27,3,27,3]{1,0,5,4,3,2:T(8,128)(2,1)} %bitcast.75) | data formatting | bytes 10077696
  133.0 112.3 %while.22 = (s32[]{:T(128)}, f32[96,1280]{1,0:T(8,128)}, s32[8,1296]{1,0:T(8,128)}, bf16[96,1280]{1,0:T(8,128)(2,1)S(1)}, bf16[8,48,27,3,27,3]{4,2,3,5,1,0:T(8,128)(2,1)}, /*index=5*/s32[]{:T(128)}, s32[]{:T(128)}) while((s32[]{:T(128)}, f32[96,1280]{1,0:T(8,128)}, s32[8,1296]{1,0:T(8,128)}, bf16[96,1280]{1,0:T(8,128)(2,1)S(1)}, ...), condition=%wide.region_5.6_spmd.clone, body=%wide.region_4.5_spmd.clone.sunk | while | flops 981762048 | bytes 10256283 | solution.py:55
  150.2 2.8 fusion.81
  164.3 2.8 fusion.81
  178.5 2.8 fusion.81
  192.7 2.8 fusion.81
  206.8 2.8 fusion.81
  221.0 2.8 fusion.81
  246.2 3.5 collective-permute-start.1
  249.6 5.1 %collective-permute-done.1 = f32[96,256]{1,0:T(8,128)S(1)} collective-permute-done((f32[96,256]{1,0:T(8,128)S(1)}, f32[96,256]{1,0:T(8,128)S(1)}, u32[]{:S(2)}, u32[]{:S(2)}) %collective-permute-start.1) | collective-permute-done | bytes 98336 | tf_op jit(solution)/shard_map/ppermute | solution.py:15
  256.3 3.6 collective-permute-done.2
  261.0 4.0 collective-permute-done.3
  265.1 3.6 collective-permute-done.4
  270.8 3.0 collective-permute-done.5
  275.4 3.0 collective-permute-done.7
  279.0 4.5 %collective-permute-done.8 = f32[2,32]{1,0:T(2,128)S(1)} collective-permute-done((f32[2,32]{1,0:T(2,128)S(1)}, f32[2,32]{1,0:T(2,128)S(1)}, u32[]{:S(2)}, u32[]{:S(2)}) %collective-permute-start.8) | collective-permute-done | bytes 288 | tf_op jit(solution)/shard_map/ppermute | solution.py:64
  288.3 3.2 collective-permute-done.9
  291.5 112.3 %while.23 = (s32[]{:T(128)}, f32[96,1280]{1,0:T(8,128)}, s32[8,1296]{1,0:T(8,128)}, bf16[96,1280]{1,0:T(8,128)(2,1)S(1)}, bf16[8,48,27,3,27,3]{4,2,3,5,1,0:T(8,128)(2,1)}, /*index=5*/s32[]{:T(128)}, s32[]{:T(128)}) while((s32[]{:T(128)}, f32[96,1280]{1,0:T(8,128)}, s32[8,1296]{1,0:T(8,128)}, bf16[96,1280]{1,0:T(8,128)(2,1)S(1)}, ...), condition=%wide.region_11.12_spmd.clone, body=%wide.region_10.11_spmd.clone.sunk | while | flops 981762048 | bytes 10256283 | solution.py:55
  351.2 2.8 fusion.89
  406.6 6.7 %collective-permute-done.10 = f32[96,256]{1,0:T(8,128)S(1)} collective-permute-done((f32[96,256]{1,0:T(8,128)S(1)}, f32[96,256]{1,0:T(8,128)S(1)}, u32[]{:S(2)}, u32[]{:S(2)}) %collective-permute-start.10) | collective-permute-done | bytes 98336 | tf_op jit(solution)/shard_map/ppermute | solution.py:15
  414.9 3.6 collective-permute-done.11
  418.9 4.7 %collective-permute-done.12 = f32[2,32]{1,0:T(2,128)S(1)} collective-permute-done((f32[2,32]{1,0:T(2,128)S(1)}, f32[2,32]{1,0:T(2,128)S(1)}, u32[]{:S(2)}, u32[]{:S(2)}) %collective-permute-start.12) | collective-permute-done | bytes 288 | tf_op jit(solution)/shard_map/ppermute | solution.py:64
  423.7 3.6 collective-permute-done.13
  429.4 3.0 collective-permute-done.14
  434.1 3.0 collective-permute-done.16
  437.7 4.5 %collective-permute-done.17 = f32[2,32]{1,0:T(2,128)S(1)} collective-permute-done((f32[2,32]{1,0:T(2,128)S(1)}, f32[2,32]{1,0:T(2,128)S(1)}, u32[]{:S(2)}, u32[]{:S(2)}) %collective-permute-start.17) | collective-permute-done | bytes 288 | tf_op jit(solution)/shard_map/ppermute | solution.py:64
  (200 shorter events, 236.2 us)
Async XLA Ops:
  5.7 12.3 %all-to-all-start = ((s32[8,1,1296]{2,1,0:T(1,128)}), s32[8,1,1296]{2,1,0:T(1,128)S(1)}, u32[]{:S(2)}, u32[]{:S(2)}) async-start(s32[8,1,1296]{2,1,0:T(1,128)} %reshape.79), calls=%async_computation | async-start | bytes 90112 | tf_op jit(solution)/shard_map/all_to_all | solution.py:85
  18.0 4.9 %copy-start = (f32[96,1024]{1,0:T(8,128)S(1)}, f32[96,1024]{1,0:T(8,128)}, u32[]{:S(2)}) copy-start(f32[96,1024]{1,0:T(8,128)} %param.8) | copy-start | bytes 1179652
  18.0 64.5 %all-to-all-start.1 = ((bf16[8,48,6656]{2,1,0:T(8,128)(2,1)}), bf16[8,48,6656]{2,1,0:T(8,128)(2,1)}, u32[]{:S(2)}, u32[]{:S(2)}) async-start(bf16[8,48,6656]{2,1,0:T(8,128)(2,1)} %bitcast.76), calls=%async_computation.1 | async-start | bytes 10223616 | tf_op jit(solution)/shard_map/all_to_all | solution.py:84
  23.0 7.5 %collective-permute-start = (bf16[96,256]{1,0:T(8,128)(2,1)S(1)}, bf16[96,256]{1,0:T(8,128)(2,1)S(1)}, u32[]{:S(2)}, u32[]{:S(2)}) collective-permute-start(bf16[96,256]{1,0:T(8,128)(2,1)S(1)} %slice.44), channel_id=1, source_target_pairs={{1,0},{2,1},{3,2},{4,3},{5,4},{6,5},{7,6},{8,7},{9,8},{10,9},{11,1... | collective-permute-start | bytes 147464 | tf_op jit(solution)/shard_map/ppermute | solution.py:15
  246.2 8.6 %collective-permute-start.1 = (f32[96,256]{1,0:T(8,128)S(1)}, f32[96,256]{1,0:T(8,128)S(1)}, u32[]{:S(2)}, u32[]{:S(2)}) collective-permute-start(f32[96,256]{1,0:T(8,128)S(1)} %slice.36), channel_id=1, source_target_pairs={{0,1},{1,2},{2,3},{3,4},{4,5},{5,6},{6,7},{7,8},{8,9},{9,10},{10,1... | collective-permute-start | bytes 294920 | tf_op jit(solution)/shard_map/ppermute | solution.py:15
  256.2 3.6 collective-permute-start.2
  259.8 5.2 %collective-permute-start.3 = (f32[2,32]{1,0:T(2,128)S(1)}, f32[2,32]{1,0:T(2,128)S(1)}, u32[]{:S(2)}, u32[]{:S(2)}) collective-permute-start(f32[2,32]{1,0:T(2,128)S(1)} %fusion.54), channel_id=1, source_target_pairs={{0,2},{1,3},{2,0},{3,1},{4,6},{5,7},{6,4},{7,5},{8,10},{9,11},{10,... | collective-permute-start | bytes 776 | tf_op jit(solution)/shard_map/ppermute | solution.py:64
  265.0 3.6 collective-permute-start.4
  268.6 5.1 %collective-permute-start.5 = (f32[2,32]{1,0:T(2,128)S(1)}, f32[2,32]{1,0:T(2,128)S(1)}, u32[]{:S(2)}, u32[]{:S(2)}) collective-permute-start(f32[2,32]{1,0:T(2,128)S(1)} %add.95), channel_id=1, source_target_pairs={{0,8},{1,9},{2,10},{3,11},{4,12},{5,13},{6,14},{7,15},{8,0},{9,1},... | collective-permute-start | bytes 776 | tf_op jit(solution)/shard_map/ppermute | solution.py:64
  273.7 1.1 collective-permute-start.6
  274.9 3.6 collective-permute-start.7
  278.4 5.1 %collective-permute-start.8 = (f32[2,32]{1,0:T(2,128)S(1)}, f32[2,32]{1,0:T(2,128)S(1)}, u32[]{:S(2)}, u32[]{:S(2)}) collective-permute-start(f32[2,32]{1,0:T(2,128)S(1)} %add.98), channel_id=1, source_target_pairs={{0,64},{1,65},{2,66},{3,67},{4,68},{5,69},{6,70},{7,71},{8,72},{9,... | collective-permute-start | bytes 776 | tf_op jit(solution)/shard_map/ppermute | solution.py:64
  285.5 6.0 %collective-permute-start.9 = (bf16[96,256]{1,0:T(8,128)(2,1)S(1)}, bf16[96,256]{1,0:T(8,128)(2,1)S(1)}, u32[]{:S(2)}, u32[]{:S(2)}) collective-permute-start(bf16[96,256]{1,0:T(8,128)(2,1)S(1)} %slice.46), channel_id=1, source_target_pairs={{1,0},{2,1},{3,2},{4,3},{5,4},{6,5},{7,6},{8,7},{9,8},{10,9},{11,1... | collective-permute-start | bytes 147464 | tf_op jit(solution)/shard_map/ppermute | solution.py:15
  404.7 8.6 %collective-permute-start.10 = (f32[96,256]{1,0:T(8,128)S(1)}, f32[96,256]{1,0:T(8,128)S(1)}, u32[]{:S(2)}, u32[]{:S(2)}) collective-permute-start(f32[96,256]{1,0:T(8,128)S(1)} %slice.41), channel_id=1, source_target_pairs={{0,1},{1,2},{2,3},{3,4},{4,5},{5,6},{6,7},{7,8},{8,9},{9,10},{10,1... | collective-permute-start | bytes 294920 | tf_op jit(solution)/shard_map/ppermute | solution.py:15
  414.8 3.6 collective-permute-start.11
  418.5 5.2 %collective-permute-start.12 = (f32[2,32]{1,0:T(2,128)S(1)}, f32[2,32]{1,0:T(2,128)S(1)}, u32[]{:S(2)}, u32[]{:S(2)}) collective-permute-start(f32[2,32]{1,0:T(2,128)S(1)} %fusion.53), channel_id=1, source_target_pairs={{0,2},{1,3},{2,0},{3,1},{4,6},{5,7},{6,4},{7,5},{8,10},{9,11},{10,... | collective-permute-start | bytes 776 | tf_op jit(solution)/shard_map/ppermute | solution.py:64
  423.6 3.6 collective-permute-start.13
  427.3 5.1 %collective-permute-start.14 = (f32[2,32]{1,0:T(2,128)S(1)}, f32[2,32]{1,0:T(2,128)S(1)}, u32[]{:S(2)}, u32[]{:S(2)}) collective-permute-start(f32[2,32]{1,0:T(2,128)S(1)} %add.104), channel_id=1, source_target_pairs={{0,8},{1,9},{2,10},{3,11},{4,12},{5,13},{6,14},{7,15},{8,0},{9,1},... | collective-permute-start | bytes 776 | tf_op jit(solution)/shard_map/ppermute | solution.py:64
  432.4 1.1 collective-permute-start.15
  433.5 3.6 collective-permute-start.16
  437.1 5.1 %collective-permute-start.17 = (f32[2,32]{1,0:T(2,128)S(1)}, f32[2,32]{1,0:T(2,128)S(1)}, u32[]{:S(2)}, u32[]{:S(2)}) collective-permute-start(f32[2,32]{1,0:T(2,128)S(1)} %add.107), channel_id=1, source_target_pairs={{0,64},{1,65},{2,66},{3,67},{4,68},{5,69},{6,70},{7,71},{8,72},{9,... | collective-permute-start | bytes 776 | tf_op jit(solution)/shard_map/ppermute | solution.py:64

commit v2 on v1

--- a/solution.py
+++ b/solution.py
@@ -30,30 +30,20 @@
     return (send_blocks.reshape(groups, capacity, -1), send_links.reshape(groups, capacity, -1))
 
 
-def window_product(matrix_groups, link_groups, field):
+def element_products(matrices, selector, field):
     rows = field.shape[0]
-    window = field.shape[1]
-    places = jnp.arange(window, dtype=jnp.int32)
-
-    def one_group(acc, pair):
-        matrix, links = pair
-        slot_count = matrix.shape[0]
-        selector = (links[:, None] == places[None, :]).astype(jnp.bfloat16)
-        picked = jnp.einsum(
-            "rw,lw->rl", field, selector, preferred_element_type=jnp.float32
-        ).astype(jnp.bfloat16)
-        picked = picked.reshape(3, rows // 3, slot_count, 27)
-        result = jnp.einsum("spcqd,cosp->dosq", matrix, picked, preferred_element_type=jnp.float32)
-        result = result.reshape(rows, slot_count * 27)
-        high_part = result.astype(jnp.bfloat16)
-        low_part = (result - high_part.astype(jnp.float32)).astype(jnp.bfloat16)
-        acc = acc + jnp.dot(high_part, selector, preferred_element_type=jnp.float32)
-        acc = acc + jnp.dot(low_part, selector, preferred_element_type=jnp.float32)
-        return (acc, None)
-
-    start = jnp.zeros((rows, window), jnp.float32)
-    acc, unused = lax.scan(one_group, start, (matrix_groups, link_groups))
-    return acc
+    count = matrices.shape[0]
+    picked = lax.dot_general(
+        selector, field, (((0,), (1,)), ((), ())), preferred_element_type=jnp.float32
+    ).astype(jnp.bfloat16)
+    picked = picked.reshape(count, 81, rows // 3)
+    result = jnp.einsum("sab,sao->sbo", matrices, picked, preferred_element_type=jnp.float32)
+    result = result.reshape(count * 27, rows)
+    high_part = result.astype(jnp.bfloat16)
+    low_part = (result - high_part.astype(jnp.float32)).astype(jnp.bfloat16)
+    acc = jnp.dot(selector, high_part, preferred_element_type=jnp.float32)
+    acc = acc + jnp.dot(selector, low_part, preferred_element_type=jnp.float32)
+    return acc.T
 
 
 def total_over_devices(value):
@@ -84,7 +74,7 @@
         lax.all_to_all(send_blocks, "grp", split_axis=0, concat_axis=0, tiled=True),
         lax.all_to_all(send_links, "grp", split_axis=0, concat_axis=0, tiled=True),
     )
-    matrix_groups = got_blocks[:, :, :6561].reshape(groups, capacity, 27, 3, 27, 3)
+    matrices = got_blocks[:, :, :6561].reshape(groups * capacity, 81, 81)
     residual = rhs
     solution = jnp.zeros(rhs.shape, jnp.float32)
     own_count = rhs.shape[1]
@@ -92,12 +82,13 @@
     local_links = jnp.clip(
         got_links - lax.axis_index("sub") * own_count, 0, own_count + band_width - 1
     ).astype(jnp.int32)
-    link_groups = local_links.reshape(groups, capacity * 27)
+    places = jnp.arange(own_count + band_width, dtype=jnp.int32)
+    selector = (places[:, None] == local_links.reshape(1, -1)).astype(jnp.bfloat16)
     for step in range(STEPS):
         rounded = residual.astype(jnp.bfloat16)
         upper = passed_along(rounded[:, :band_width], "sub", -1)
         field = jnp.concatenate([rounded, upper], axis=1)
-        partial_sum = window_product(matrix_groups, link_groups, field)
+        partial_sum = element_products(matrices, selector, field)
         incoming = passed_along(partial_sum[:, own_count:], "sub", 1)
         image = partial_sum[:, :own_count] + jnp.pad(
             incoming, ((0, 0), (0, own_count - band_width))

time: 448 us -> 320 us (0.71)
  local copies, waits for them, and re-layouts: 141 us -> 72.7 us
  matrix products: 147 us -> 112 us
  waiting for transfers between devices: 113 us -> 90.5 us
  other arithmetic: 9.93 us -> 4.9 us
    unnamed x7 -> x5, local copies, waits for them, and re-layouts: 52.2 us -> 1.7 us
    dot_general x64 -> x8, matrix products: 147 us -> 112 us  [the longest x2 33 us: element_products(): jnp.einsum('sab,sao->sbo', matrices, picked, preferred_element_type=jnp.f...]
    all_to_all x1, waiting for transfers between devices: 52.1 us -> 29.5 us  [shards(): lax.all_to_all(send_blocks, 'grp', split_axis=0, concat_axis=0, tiled=True)]
    transpose x16 -> x0, local copies, waits for them, and re-layouts: 21.9 us -> none  [one_group(): jnp.einsum('spcqd,cosp->dosq', matrix, picked, preferred_element_type=jnp...]
    dynamic_slice x16 -> x0, local copies, waits for them, and re-layouts: 13 us -> none  [window_product(): acc, unused = lax.scan(one_group, start, (matrix_groups, link_groups))]
    reshape x33 -> x5, local copies, waits for them, and re-layouts: 43.3 us -> 55.5 us  [the longest x2 24.5 us: element_products(): result = result.reshape(count * 27, rows)]
    convert_element_type x0 -> x2, local copies, waits for them, and re-layouts: none -> 6.09 us  [element_products(): picked = lax.dot_general(selector, field, (((0,), (1,)), ((), ())), prefe...]
  transfers between devices with their start and end apart: 20 -> 20, of which waited for: 18 -> 18; matrix products, arithmetic and copies ran while one was open for 2% -> 10% of each run, Pallas kernels for 0% -> 0%
where the time goes in v2:
time: 320 us; the launch traced here: 313 us
  matrix products  112 us (35%)
  waiting for transfers between devices  90.5 us (28%)
  local copies, waits for them, and re-layouts  72.7 us (23%)
  starting transfers between devices  31.9 us (10%)
  other arithmetic  4.9 us (2%)
    ppermute x14, waiting for transfers between devices, total_over_devices(): value = value + lax.ppermute(value, axes, pairs)  46 us
    dot_general x2, matrix products, element_products(): jnp.einsum('sab,sao->sbo', matrices, picked, preferred_element_type=jnp.f...  33 us
    dot_general x2, matrix products, element_products(): acc = acc + jnp.dot(selector, low_part, preferred_element_type=jnp.float32)  29.9 us
    all_to_all x1, waiting for transfers between devices, shards(): lax.all_to_all(send_blocks, 'grp', split_axis=0, concat_axis=0, tiled=True)  29.5 us
    dot_general x2, matrix products, element_products(): acc = jnp.dot(selector, high_part, preferred_element_type=jnp.float32)  25.8 us
    reshape x2, local copies, waits for them, and re-layouts, element_products(): result = result.reshape(count * 27, rows)  24.5 us
    dot_general x2, matrix products, element_products(): lax.dot_general(selector, field, (((0,), (1,)), ((), ())), preferred_elem...  23.5 us
    reshape x2, local copies, waits for them, and re-layouts, element_products(): picked = picked.reshape(count, 81, rows // 3)  17 us
  transfers between devices with their start and end apart: 20, of which 18 were waited for; matrix products, arithmetic and copies ran while one was open for 10% of the time, Pallas kernels for 0%

profile of v2, /device:TPU:2, one launch (start us, length us, event | category | flops | bytes accessed | tf_op | source)
XLA Modules:
  0.0 313.3 jit_solution(5843108519495238145)
XLA Ops:
  5.7 5.3 %all-to-all-start.1 = ((s32[8,1,1296]{2,1,0:T(1,128)}), s32[8,1,1296]{2,1,0:T(1,128)S(1)}, u32[]{:S(2)}, u32[]{:S(2)}) async-start(s32[8,1,1296]{2,1,0:T(1,128)} %reshape.65), calls=%async_computation.1 | async-start | bytes 90112 | tf_op jit(solution)/shard_map/all_to_all | solution.py:75
  11.0 6.9 %scatter_custom_fusion = bf16[384,6656]{1,0:T(8,128)(2,1)} fusion(s32[128]{0:T(128)S(1)} %fusion.32, bf16[128,6656]{1,0:T(8,128)(2,1)} %param.5, bf16[]{:T(256)} %constant.9.clone.1), kind=kCustom, calls=%fused_computation.19 | custom fusion | bytes 5112320 | tf_op jit(solution)/shard_map/scatter | solution.py:27
  18.0 4.9 %all-to-all-start = ((bf16[8,48,6656]{2,1,0:T(8,128)(2,1)}), bf16[8,48,6656]{2,1,0:T(8,128)(2,1)}, u32[]{:S(2)}, u32[]{:S(2)}) async-start(bf16[8,48,6656]{2,1,0:T(8,128)(2,1)} %bitcast.26), calls=%async_computation | async-start | bytes 10223616 | tf_op jit(solution)/shard_map/all_to_all | solution.py:74
  23.0 4.9 %collective-permute-start = (bf16[96,256]{1,0:T(8,128)(2,1)S(1)}, bf16[96,256]{1,0:T(8,128)(2,1)S(1)}, u32[]{:S(2)}, u32[]{:S(2)}) collective-permute-start(bf16[96,256]{1,0:T(8,128)(2,1)S(1)} %slice.45), channel_id=1, source_target_pairs={{1,0},{2,1},{3,2},{4,3},{5,4},{6,5},{7,6},{8,7},{9,8},{10,9},{11,1... | collective-permute-start | bytes 147464 | tf_op jit(solution)/shard_map/ppermute | solution.py:15
  29.7 11.8 %fusion.12 = bf16[10368,96]{0,1:T(8,128)(2,1)} fusion(s32[10368]{0:T(1024)S(1)} %eq.35, bf16[96,256]{1,0:T(8,128)(2,1)S(1)} %collective-permute-done, bf16[96,1024]{1,0:T(8,128)(2,1)S(1)} %convert_element_type.38), kind=kOutput, calls=%fused_computation.15 | convolution fusion | flops 2562797568 | bytes 2277888 | tf_op jit(solution)/shard_map/dot_general | solution.py:36
  41.5 3.0 copy.26
  44.5 8.5 %reshape.41 = bf16[384,81,32]{2,1,0:T(8,128)(2,1)} reshape(bf16[10368,96]{1,0:T(8,128)(2,1)S(1)} %copy.26) | data formatting | bytes 3981312 | tf_op jit(solution)/shard_map/reshape | solution.py:39
  53.1 29.5 %all-to-all-done = bf16[8,48,6656]{2,1,0:T(8,128)(2,1)} async-done(((bf16[8,48,6656]{2,1,0:T(8,128)(2,1)}), bf16[8,48,6656]{2,1,0:T(8,128)(2,1)}, u32[]{:S(2)}, u32[]{:S(2)}) %all-to-all-start) | async-done | bytes 5111840 | tf_op jit(solution)/shard_map/all_to_all | solution.py:74
  82.5 14.0 %reshape.39 = bf16[384,81,81]{2,1,0:T(8,128)(2,1)} reshape(bf16[8,48,6561]{2,1,0:T(8,128)(2,1)} %bitcast.23) | data formatting | bytes 10077696 | tf_op jit(solution)/shard_map/reshape | solution.py:77
  96.5 16.5 %fusion.40 = f32[384,81,32]{2,1,0:T(8,128)} fusion(bf16[384,81,81]{2,1,0:T(8,128)(2,1)} %reshape.39, bf16[384,81,32]{2,1,0:T(8,128)(2,1)} %reshape.41), kind=kOutput, calls=%fused_computation.63 | convolution fusion | flops 161243136 | bytes 11010816 | tf_op jit(solution)/shard_map/sab,sao->sbo/dot_general | solution.py:40
  113.0 12.2 %reshape.42 = f32[10368,96]{1,0:T(8,128)} reshape(f32[384,81,32]{2,1,0:T(8,128)} %fusion.40) | data formatting | bytes 7962624 | tf_op jit(solution)/shard_map/reshape | solution.py:41
  125.2 12.9 %fusion.4 = f32[96,1280]{1,0:T(8,128)S(1)} fusion(s32[10368]{0:T(1024)S(1)} %eq.35, f32[10368,96]{1,0:T(8,128)} %reshape.42), kind=kOutput, calls=%fused_computation.7 | convolution fusion | flops 2562306048 | bytes 4514304 | tf_op jit(solution)/shard_map/dot_general | solution.py:44
  138.2 15.0 %fusion.16 = f32[96,1280]{1,0:T(8,128)S(1)} fusion(f32[96,1280]{1,0:T(8,128)S(1)} %fusion.4, s32[10368]{0:T(1024)S(1)} %eq.35, f32[10368,96]{1,0:T(8,128)} %reshape.42), kind=kOutput, calls=%fused_computation.21 | convolution fusion | flops 2565414912 | bytes 5005824 | tf_op jit(solution)/shard_map/dot_general | solution.py:45
  153.2 3.5 %collective-permute-start.1 = (f32[96,256]{1,0:T(8,128)S(1)}, f32[96,256]{1,0:T(8,128)S(1)}, u32[]{:S(2)}, u32[]{:S(2)}) collective-permute-start(f32[96,256]{1,0:T(8,128)S(1)} %slice.47), channel_id=1, source_target_pairs={{0,1},{1,2},{2,3},{3,4},{4,5},{5,6},{6,7},{7,8},{8,9},{9,10},{10,1... | collective-permute-start | bytes 294920 | tf_op jit(solution)/shard_map/ppermute | solution.py:15
  156.7 5.1 %collective-permute-done.1 = f32[96,256]{1,0:T(8,128)S(1)} collective-permute-done((f32[96,256]{1,0:T(8,128)S(1)}, f32[96,256]{1,0:T(8,128)S(1)}, u32[]{:S(2)}, u32[]{:S(2)}) %collective-permute-start.1) | collective-permute-done | bytes 98336 | tf_op jit(solution)/shard_map/ppermute | solution.py:15
  162.2 3.6 %collective-permute-done.2 = f32[2,32]{1,0:T(2,128)S(1)} collective-permute-done((f32[2,32]{1,0:T(2,128)S(1)}, f32[2,32]{1,0:T(2,128)S(1)}, u32[]{:S(2)}, u32[]{:S(2)}) %collective-permute-start.2) | collective-permute-done | bytes 288 | tf_op jit(solution)/shard_map/ppermute | solution.py:54
  167.0 4.0 %collective-permute-done.3 = f32[2,32]{1,0:T(2,128)S(1)} collective-permute-done((f32[2,32]{1,0:T(2,128)S(1)}, f32[2,32]{1,0:T(2,128)S(1)}, u32[]{:S(2)}, u32[]{:S(2)}) %collective-permute-start.3) | collective-permute-done | bytes 288 | tf_op jit(solution)/shard_map/ppermute | solution.py:54
  171.1 3.6 %collective-permute-done.4 = f32[2,32]{1,0:T(2,128)S(1)} collective-permute-done((f32[2,32]{1,0:T(2,128)S(1)}, f32[2,32]{1,0:T(2,128)S(1)}, u32[]{:S(2)}, u32[]{:S(2)}) %collective-permute-start.4) | collective-permute-done | bytes 288 | tf_op jit(solution)/shard_map/ppermute | solution.py:54
  185.0 4.5 %collective-permute-done.8 = f32[2,32]{1,0:T(2,128)S(1)} collective-permute-done((f32[2,32]{1,0:T(2,128)S(1)}, f32[2,32]{1,0:T(2,128)S(1)}, u32[]{:S(2)}, u32[]{:S(2)}) %collective-permute-start.8) | collective-permute-done | bytes 288 | tf_op jit(solution)/shard_map/ppermute | solution.py:54
  192.5 3.2 %collective-permute-done.9 = bf16[96,256]{1,0:T(8,128)(2,1)S(1)} collective-permute-done((bf16[96,256]{1,0:T(8,128)(2,1)S(1)}, bf16[96,256]{1,0:T(8,128)(2,1)S(1)}, u32[]{:S(2)}, u32[]{:S(2)}) %collective-permute-start.9) | collective-permute-done | bytes 49184 | tf_op jit(solution)/shard_map/ppermute | solution.py:15
  195.7 11.7 %fusion.13 = bf16[10368,96]{0,1:T(8,128)(2,1)} fusion(s32[10368]{0:T(1024)S(1)} %eq.35, bf16[96,256]{1,0:T(8,128)(2,1)S(1)} %collective-permute-done.9, bf16[96,1024]{1,0:T(8,128)(2,1)S(1)} %get-tuple-element.6), kind=kOutput, calls=%fused_computation.16 | convolution fusion | flops 2562797568 | bytes 2277888 | tf_op jit(solution)/shard_map/dot_general | solution.py:36
  207.4 3.0 copy.29
  210.5 8.5 %reshape.43 = bf16[384,81,32]{2,1,0:T(8,128)(2,1)} reshape(bf16[10368,96]{1,0:T(8,128)(2,1)S(1)} %copy.29) | data formatting | bytes 3981312 | tf_op jit(solution)/shard_map/reshape | solution.py:39
  219.0 16.5 %fusion.41 = f32[384,81,32]{2,1,0:T(8,128)} fusion(bf16[384,81,81]{2,1,0:T(8,128)(2,1)} %reshape.39, bf16[384,81,32]{2,1,0:T(8,128)(2,1)} %reshape.43), kind=kOutput, calls=%fused_computation.64 | convolution fusion | flops 161243136 | bytes 11010816 | tf_op jit(solution)/shard_map/sab,sao->sbo/dot_general | solution.py:40
  235.5 12.2 %reshape.44 = f32[10368,96]{1,0:T(8,128)} reshape(f32[384,81,32]{2,1,0:T(8,128)} %fusion.41) | data formatting | bytes 7962624 | tf_op jit(solution)/shard_map/reshape | solution.py:41
  247.7 12.9 %fusion.1 = f32[96,1280]{1,0:T(8,128)S(1)} fusion(s32[10368]{0:T(1024)S(1)} %eq.35, f32[10368,96]{1,0:T(8,128)} %reshape.44), kind=kOutput, calls=%fused_computation.4 | convolution fusion | flops 2562306048 | bytes 4514304 | tf_op jit(solution)/shard_map/dot_general | solution.py:44
  260.6 15.0 %fusion.17 = f32[96,1280]{1,0:T(8,128)S(1)} fusion(f32[96,1280]{1,0:T(8,128)S(1)} %fusion.1, s32[10368]{0:T(1024)S(1)} %eq.35, f32[10368,96]{1,0:T(8,128)} %reshape.44), kind=kOutput, calls=%fused_computation.22 | convolution fusion | flops 2565414912 | bytes 5005824 | tf_op jit(solution)/shard_map/dot_general | solution.py:45
  277.6 6.7 %collective-permute-done.10 = f32[96,256]{1,0:T(8,128)S(1)} collective-permute-done((f32[96,256]{1,0:T(8,128)S(1)}, f32[96,256]{1,0:T(8,128)S(1)}, u32[]{:S(2)}, u32[]{:S(2)}) %collective-permute-start.10) | collective-permute-done | bytes 98336 | tf_op jit(solution)/shard_map/ppermute | solution.py:15
  284.7 3.6 %collective-permute-done.11 = f32[2,32]{1,0:T(2,128)S(1)} collective-permute-done((f32[2,32]{1,0:T(2,128)S(1)}, f32[2,32]{1,0:T(2,128)S(1)}, u32[]{:S(2)}, u32[]{:S(2)}) %collective-permute-start.11) | collective-permute-done | bytes 288 | tf_op jit(solution)/shard_map/ppermute | solution.py:54
  288.7 4.7 %collective-permute-done.12 = f32[2,32]{1,0:T(2,128)S(1)} collective-permute-done((f32[2,32]{1,0:T(2,128)S(1)}, f32[2,32]{1,0:T(2,128)S(1)}, u32[]{:S(2)}, u32[]{:S(2)}) %collective-permute-start.12) | collective-permute-done | bytes 288 | tf_op jit(solution)/shard_map/ppermute | solution.py:54
  293.5 3.6 %collective-permute-done.13 = f32[2,32]{1,0:T(2,128)S(1)} collective-permute-done((f32[2,32]{1,0:T(2,128)S(1)}, f32[2,32]{1,0:T(2,128)S(1)}, u32[]{:S(2)}, u32[]{:S(2)}) %collective-permute-start.13) | collective-permute-done | bytes 288 | tf_op jit(solution)/shard_map/ppermute | solution.py:54
  307.5 4.5 %collective-permute-done.17 = f32[2,32]{1,0:T(2,128)S(1)} collective-permute-done((f32[2,32]{1,0:T(2,128)S(1)}, f32[2,32]{1,0:T(2,128)S(1)}, u32[]{:S(2)}, u32[]{:S(2)}) %collective-permute-start.17) | collective-permute-done | bytes 288 | tf_op jit(solution)/shard_map/ppermute | solution.py:54
  (79 shorter events, 36.5 us)
Async XLA Ops:
  5.7 12.3 %all-to-all-start.1 = ((s32[8,1,1296]{2,1,0:T(1,128)}), s32[8,1,1296]{2,1,0:T(1,128)S(1)}, u32[]{:S(2)}, u32[]{:S(2)}) async-start(s32[8,1,1296]{2,1,0:T(1,128)} %reshape.65), calls=%async_computation.1 | async-start | bytes 90112 | tf_op jit(solution)/shard_map/all_to_all | solution.py:75
  18.0 4.9 %copy-start = (f32[96,1024]{1,0:T(8,128)S(1)}, f32[96,1024]{1,0:T(8,128)}, u32[]{:S(2)}) copy-start(f32[96,1024]{1,0:T(8,128)} %param.4) | copy-start | bytes 1179652
  18.0 64.5 %all-to-all-start = ((bf16[8,48,6656]{2,1,0:T(8,128)(2,1)}), bf16[8,48,6656]{2,1,0:T(8,128)(2,1)}, u32[]{:S(2)}, u32[]{:S(2)}) async-start(bf16[8,48,6656]{2,1,0:T(8,128)(2,1)} %bitcast.26), calls=%async_computation | async-start | bytes 10223616 | tf_op jit(solution)/shard_map/all_to_all | solution.py:74
  23.0 6.7 %collective-permute-start = (bf16[96,256]{1,0:T(8,128)(2,1)S(1)}, bf16[96,256]{1,0:T(8,128)(2,1)S(1)}, u32[]{:S(2)}, u32[]{:S(2)}) collective-permute-start(bf16[96,256]{1,0:T(8,128)(2,1)S(1)} %slice.45), channel_id=1, source_target_pairs={{1,0},{2,1},{3,2},{4,3},{5,4},{6,5},{7,6},{8,7},{9,8},{10,9},{11,1... | collective-permute-start | bytes 147464 | tf_op jit(solution)/shard_map/ppermute | solution.py:15
  153.2 8.6 %collective-permute-start.1 = (f32[96,256]{1,0:T(8,128)S(1)}, f32[96,256]{1,0:T(8,128)S(1)}, u32[]{:S(2)}, u32[]{:S(2)}) collective-permute-start(f32[96,256]{1,0:T(8,128)S(1)} %slice.47), channel_id=1, source_target_pairs={{0,1},{1,2},{2,3},{3,4},{4,5},{5,6},{6,7},{7,8},{8,9},{9,10},{10,1... | collective-permute-start | bytes 294920 | tf_op jit(solution)/shard_map/ppermute | solution.py:15
  162.2 3.6 %collective-permute-start.2 = (f32[2,32]{1,0:T(2,128)S(1)}, f32[2,32]{1,0:T(2,128)S(1)}, u32[]{:S(2)}, u32[]{:S(2)}) collective-permute-start(f32[2,32]{1,0:T(2,128)S(1)} %pad_maximum_fusion), channel_id=1, source_target_pairs={{0,1},{1,0},{2,3},{3,2},{4,5},{5,4},{6,7},{7,6},{8,9},{9,8},{10,11... | collective-permute-start | bytes 776 | tf_op jit(solution)/shard_map/ppermute | solution.py:54
  165.8 5.2 %collective-permute-start.3 = (f32[2,32]{1,0:T(2,128)S(1)}, f32[2,32]{1,0:T(2,128)S(1)}, u32[]{:S(2)}, u32[]{:S(2)}) collective-permute-start(f32[2,32]{1,0:T(2,128)S(1)} %fusion.38), channel_id=1, source_target_pairs={{0,2},{1,3},{2,0},{3,1},{4,6},{5,7},{6,4},{7,5},{8,10},{9,11},{10,... | collective-permute-start | bytes 776 | tf_op jit(solution)/shard_map/ppermute | solution.py:54
  171.0 3.6 %collective-permute-start.4 = (f32[2,32]{1,0:T(2,128)S(1)}, f32[2,32]{1,0:T(2,128)S(1)}, u32[]{:S(2)}, u32[]{:S(2)}) collective-permute-start(f32[2,32]{1,0:T(2,128)S(1)} %fusion.47), channel_id=1, source_target_pairs={{0,4},{1,5},{2,6},{3,7},{4,0},{5,1},{6,2},{7,3},{8,12},{9,13},{10,... | collective-permute-start | bytes 776 | tf_op jit(solution)/shard_map/ppermute | solution.py:54
  174.6 5.1 %collective-permute-start.5 = (f32[2,32]{1,0:T(2,128)S(1)}, f32[2,32]{1,0:T(2,128)S(1)}, u32[]{:S(2)}, u32[]{:S(2)}) collective-permute-start(f32[2,32]{1,0:T(2,128)S(1)} %add.86), channel_id=1, source_target_pairs={{0,8},{1,9},{2,10},{3,11},{4,12},{5,13},{6,14},{7,15},{8,0},{9,1},... | collective-permute-start | bytes 776 | tf_op jit(solution)/shard_map/ppermute | solution.py:54
  179.7 1.1 collective-permute-start.6
  180.9 3.6 %collective-permute-start.7 = (f32[2,32]{1,0:T(2,128)S(1)}, f32[2,32]{1,0:T(2,128)S(1)}, u32[]{:S(2)}, u32[]{:S(2)}) collective-permute-start(f32[2,32]{1,0:T(2,128)S(1)} %add.88), channel_id=1, source_target_pairs={{0,32},{1,33},{2,34},{3,35},{4,36},{5,37},{6,38},{7,39},{8,40},{9,... | collective-permute-start | bytes 776 | tf_op jit(solution)/shard_map/ppermute | solution.py:54
  184.4 5.1 %collective-permute-start.8 = (f32[2,32]{1,0:T(2,128)S(1)}, f32[2,32]{1,0:T(2,128)S(1)}, u32[]{:S(2)}, u32[]{:S(2)}) collective-permute-start(f32[2,32]{1,0:T(2,128)S(1)} %add.89), channel_id=1, source_target_pairs={{0,64},{1,65},{2,66},{3,67},{4,68},{5,69},{6,70},{7,71},{8,72},{9,... | collective-permute-start | bytes 776 | tf_op jit(solution)/shard_map/ppermute | solution.py:54
  189.7 6.0 %collective-permute-start.9 = (bf16[96,256]{1,0:T(8,128)(2,1)S(1)}, bf16[96,256]{1,0:T(8,128)(2,1)S(1)}, u32[]{:S(2)}, u32[]{:S(2)}) collective-permute-start(bf16[96,256]{1,0:T(8,128)(2,1)S(1)} %slice.48), channel_id=1, source_target_pairs={{1,0},{2,1},{3,2},{4,3},{5,4},{6,5},{7,6},{8,7},{9,8},{10,9},{11,1... | collective-permute-start | bytes 147464 | tf_op jit(solution)/shard_map/ppermute | solution.py:15
  275.6 8.6 %collective-permute-start.10 = (f32[96,256]{1,0:T(8,128)S(1)}, f32[96,256]{1,0:T(8,128)S(1)}, u32[]{:S(2)}, u32[]{:S(2)}) collective-permute-start(f32[96,256]{1,0:T(8,128)S(1)} %slice.50), channel_id=1, source_target_pairs={{0,1},{1,2},{2,3},{3,4},{4,5},{5,6},{6,7},{7,8},{8,9},{9,10},{10,1... | collective-permute-start | bytes 294920 | tf_op jit(solution)/shard_map/ppermute | solution.py:15
  284.6 3.6 %collective-permute-start.11 = (f32[2,32]{1,0:T(2,128)S(1)}, f32[2,32]{1,0:T(2,128)S(1)}, u32[]{:S(2)}, u32[]{:S(2)}) collective-permute-start(f32[2,32]{1,0:T(2,128)S(1)} %pad_maximum_fusion.1), channel_id=1, source_target_pairs={{0,1},{1,0},{2,3},{3,2},{4,5},{5,4},{6,7},{7,6},{8,9},{9,8},{10,11... | collective-permute-start | bytes 776 | tf_op jit(solution)/shard_map/ppermute | solution.py:54
  288.3 5.2 %collective-permute-start.12 = (f32[2,32]{1,0:T(2,128)S(1)}, f32[2,32]{1,0:T(2,128)S(1)}, u32[]{:S(2)}, u32[]{:S(2)}) collective-permute-start(f32[2,32]{1,0:T(2,128)S(1)} %fusion.37), channel_id=1, source_target_pairs={{0,2},{1,3},{2,0},{3,1},{4,6},{5,7},{6,4},{7,5},{8,10},{9,11},{10,... | collective-permute-start | bytes 776 | tf_op jit(solution)/shard_map/ppermute | solution.py:54
  293.4 3.6 %collective-permute-start.13 = (f32[2,32]{1,0:T(2,128)S(1)}, f32[2,32]{1,0:T(2,128)S(1)}, u32[]{:S(2)}, u32[]{:S(2)}) collective-permute-start(f32[2,32]{1,0:T(2,128)S(1)} %fusion.46), channel_id=1, source_target_pairs={{0,4},{1,5},{2,6},{3,7},{4,0},{5,1},{6,2},{7,3},{8,12},{9,13},{10,... | collective-permute-start | bytes 776 | tf_op jit(solution)/shard_map/ppermute | solution.py:54
  297.1 5.1 %collective-permute-start.14 = (f32[2,32]{1,0:T(2,128)S(1)}, f32[2,32]{1,0:T(2,128)S(1)}, u32[]{:S(2)}, u32[]{:S(2)}) collective-permute-start(f32[2,32]{1,0:T(2,128)S(1)} %add.96), channel_id=1, source_target_pairs={{0,8},{1,9},{2,10},{3,11},{4,12},{5,13},{6,14},{7,15},{8,0},{9,1},... | collective-permute-start | bytes 776 | tf_op jit(solution)/shard_map/ppermute | solution.py:54
  302.2 1.1 collective-permute-start.15
  303.3 3.6 %collective-permute-start.16 = (f32[2,32]{1,0:T(2,128)S(1)}, f32[2,32]{1,0:T(2,128)S(1)}, u32[]{:S(2)}, u32[]{:S(2)}) collective-permute-start(f32[2,32]{1,0:T(2,128)S(1)} %add.98), channel_id=1, source_target_pairs={{0,32},{1,33},{2,34},{3,35},{4,36},{5,37},{6,38},{7,39},{8,40},{9,... | collective-permute-start | bytes 776 | tf_op jit(solution)/shard_map/ppermute | solution.py:54
  306.9 5.1 %collective-permute-start.17 = (f32[2,32]{1,0:T(2,128)S(1)}, f32[2,32]{1,0:T(2,128)S(1)}, u32[]{:S(2)}, u32[]{:S(2)}) collective-permute-start(f32[2,32]{1,0:T(2,128)S(1)} %add.99), channel_id=1, source_target_pairs={{0,64},{1,65},{2,66},{3,67},{4,68},{5,69},{6,70},{7,71},{8,72},{9,... | collective-permute-start | bytes 776 | tf_op jit(solution)/shard_map/ppermute | solution.py:54
